TPU v7x, 128 devices: a whole 4x4x4 slice. The times are simulated.
128 devices in a mesh: seq: 16 (over y, z), batch: 8 (over x, core).
Axes of the slice: x: 4, y: 4, z: 4, core: 2. Of those that a mesh axis runs over, the one named last changes fastest.
Arguments:
- q_nope: bfloat16 [8, 64, 128, 128], P('batch', None, 'seq'), may hold values from -6 to 6
- q_rope: bfloat16 [8, 64, 128, 64], P('batch', None, 'seq'), may hold values from -8 to 8
- absorb_k: bfloat16 [128, 128, 512], P('seq'), may hold values from -0.5 to 0.5
- absorb_v: bfloat16 [128, 512, 128], P('seq'), may hold values from -0.25 to 0.25
- cache_latent: bfloat16 [8, 16384, 512], P('batch', 'seq'), may hold values from -6 to 6
- cache_rope: bfloat16 [8, 16384, 64], P('batch', 'seq'), may hold values from -8 to 8
- draft_latent: bfloat16 [8, 64, 512], P('batch'), may hold values from -6 to 6
- draft_rope: bfloat16 [8, 64, 64], P('batch'), may hold values from -6 to 6
- residual: bfloat16 [512, 7168], P('batch', 'seq'), may hold values from -1.2 to 1.2
- out_proj: bfloat16 [16384, 7168], P('seq'), may hold values from -0.046875 to 0.046875
- norm_gain: float32 [7168], replicated, may hold values from 0.5 to 1.5
- lm_head: bfloat16 [65536, 7168], P(('seq', 'batch')), may hold values from -2.4095235 to 2.4095235
- parent: int32 [8, 64], replicated, may hold values from 0 to 62, as said below
- draft_ids: int32 [8, 64], replicated, may hold values from 0 to 65535
- cache_len: int32 [8], P('batch'), may hold values from 4096 to 16384
- accept_len: int32 [8], P('batch'), may hold values from 1 to 64
Outputs:
- hidden_out: bfloat16 [512, 7168], P('batch', 'seq')
- target_logp: float32 [8, 64], P('batch')
- accepted_score: float32 [8], P('batch')
Inputs may be any that keep to these rules, and one draw needn't show every extreme that they name: parent[b, 0] = 0, and 0 <= parent[b, i] < i for i >= 1.
All inputs are finite; a program needn't handle non-finite values.
Results may differ from a plain program's by a relative error of at most 0.0095.
Values may be sent and summed in bfloat16 or wider, within the bound.
A program may use at most 256 MiB of HBM per device.

v0:
```python
import math
import jax
import jax.numpy as jnp
from jax import lax
from jax.sharding import Mesh
from jax.sharding import PartitionSpec as P

SEQ = ("seq_0", "seq_1")
BATCH = ("batch_0", "batch_1")
SEQ_BATCH = ("seq_0", "seq_1", "batch_0", "batch_1")
masked_value = -1e30
norm_epsilon = 1e-06
highest = lax.Precision.HIGHEST


def sent_together(arrays, axis, dim, along):
    ends, at = ([], 0)
    for a in arrays[:-1]:
        at += a.shape[along]
        ends.append(at)
    both = jnp.concatenate(arrays, axis=along)
    return tuple(jnp.split(lax.all_gather(both, axis, axis=dim, tiled=True), ends, axis=along))


def copy_for_each(array, axis):
    copies = jnp.broadcast_to(array, (lax.axis_size(axis), *array.shape))
    return lax.all_to_all(copies, axis, split_axis=0, concat_axis=0, tiled=True)


def over_copies(array, axis):
    everything = copy_for_each(array, axis)
    return jnp.max(everything, axis=0)


def gathered_once(array, axis):
    leaves = jax.tree.leaves(array)
    sequence = sorted(range(len(leaves)), key=lambda k: -leaves[k].size)
    width = (1, *leaves[sequence[0]].shape)[-1]
    lines = [
        jnp.pad(leaves[k].reshape(-1), (0, -leaves[k].size % width)).reshape(-1, width)
        for k in sequence
    ]
    both, at, found = (lax.all_gather(jnp.concatenate(lines), axis), 0, {})
    for k, line in zip(sequence, lines):
        piece = both[:, at : at + len(line)].reshape(len(both), -1)
        found[k] = piece[:, : leaves[k].size].reshape(-1, *leaves[k].shape)
        at += len(line)
    numbers = iter(range(len(leaves)))
    return jax.tree.map(lambda _: found[next(numbers)], array)


def combined_by_axis(array, axes, combine):
    for axis in axes:
        pieces = gathered_once(array, axis)
        array = jax.tree.map(lambda part: part[0], pieces)
        for k in range(1, lax.axis_size(axis)):
            array = combine(array, jax.tree.map(lambda part: part[k], pieces))
    return array


def ancestry_of(parents):
    draft_count = parents.shape[1]
    indices = jnp.arange(draft_count, dtype=jnp.int32)
    parent_map = (
        (parents[:, :, None] == indices[None, None, :]) & (indices[None, :, None] > 0)
    ).astype(jnp.float32)
    ancestry = jnp.broadcast_to(jnp.eye(draft_count, dtype=jnp.float32), parent_map.shape)
    for doubling in range(draft_count.bit_length() - 1):
        ancestry = ancestry + jnp.einsum("rij,rjk->rik", ancestry, parent_map, precision=highest)
        parent_map = jnp.einsum("rij,rjk->rik", parent_map, parent_map, precision=highest)
    return ancestry > 0.5


def combine_soft(earlier, later):
    top_new = jnp.maximum(earlier[0], later[0])
    mass_new = earlier[1] * jnp.exp(earlier[0] - top_new) + later[1] * jnp.exp(later[0] - top_new)
    return (top_new, mass_new, earlier[2] + later[2])


def body(
    q_nope,
    q_rope,
    absorb_k,
    absorb_v,
    cache_latent,
    cache_rope,
    draft_latent,
    draft_rope,
    residual,
    out_proj,
    norm_gain,
    lm_head,
    parent,
    draft_ids,
    cache_len,
    accept_len,
):
    requests, draft_count, local_heads, nope_width = q_nope.shape
    cache_rows = cache_latent.shape[1]
    score_scale = 1.0 / math.sqrt(nope_width + q_rope.shape[3])
    seq_index = lax.axis_index(SEQ)
    batch_index = lax.axis_index(BATCH)
    query_latent = jnp.einsum(
        "rihn,hnc->rihc", q_nope, absorb_k, preferred_element_type=jnp.float32
    ).astype(jnp.bfloat16)
    query_all, rope_all = sent_together((query_latent, q_rope), SEQ, 2, 3)
    cache_scores = jnp.einsum(
        "rihc,rtc->rhit", query_all, cache_latent, preferred_element_type=jnp.float32
    )
    cache_scores = cache_scores + jnp.einsum(
        "rihe,rte->rhit", rope_all, cache_rope, preferred_element_type=jnp.float32
    )
    positions = seq_index * cache_rows + jnp.arange(cache_rows, dtype=jnp.int32)
    in_cache = positions[None, :] < cache_len[:, None]
    cache_scores = jnp.where(in_cache[:, None, None, :], cache_scores * score_scale, masked_value)
    tree_scores = jnp.einsum(
        "rihc,rjc->rhij", query_all, draft_latent, preferred_element_type=jnp.float32
    )
    tree_scores = tree_scores + jnp.einsum(
        "rihe,rje->rhij", rope_all, draft_rope, preferred_element_type=jnp.float32
    )
    own_parents = lax.dynamic_slice_in_dim(parent, batch_index * requests, requests, 0)
    ancestry = ancestry_of(own_parents)
    tree_scores = jnp.where(ancestry[:, None, :, :], tree_scores * score_scale, masked_value)
    local_top = jnp.maximum(jnp.max(cache_scores, axis=3), jnp.max(tree_scores, axis=3))
    row_top = over_copies(local_top, SEQ)
    cache_weights = jnp.exp(cache_scores - row_top[..., None])
    weight_sum = jnp.sum(cache_weights, axis=3)
    partial_value = jnp.einsum(
        "rhit,rtc->rhic",
        cache_weights.astype(jnp.bfloat16),
        cache_latent,
        preferred_element_type=jnp.float32,
    )
    head_first = seq_index * local_heads
    tree_mine = lax.dynamic_slice_in_dim(tree_scores, head_first, local_heads, 1)
    top_mine = lax.dynamic_slice_in_dim(row_top, head_first, local_heads, 1)
    tree_weights = jnp.exp(tree_mine - top_mine[..., None])
    tree_out = jnp.einsum(
        "rhij,rjc->rhic",
        tree_weights.astype(jnp.bfloat16),
        draft_latent,
        preferred_element_type=jnp.float32,
    )
    latent_sum, weight_total = (
        lax.psum_scatter(partial_value, SEQ, scatter_dimension=1, tiled=True),
        lax.psum_scatter(weight_sum, SEQ, scatter_dimension=1, tiled=True),
    )
    summed = jnp.einsum(
        "rhic,hcn->rhin", latent_sum + tree_out, absorb_v, preferred_element_type=jnp.float32
    )
    weight_total = weight_total + jnp.sum(tree_weights, axis=3)
    head_out = (summed / weight_total[..., None]).astype(jnp.bfloat16)
    head_rows = jnp.transpose(head_out, (0, 2, 1, 3)).reshape(
        requests * draft_count, local_heads * head_out.shape[3]
    )
    branch_term = jnp.dot(head_rows, out_proj, preferred_element_type=jnp.float32)
    width_local = residual.shape[1]
    feature_first = seq_index * width_local
    residual_wide = lax.dynamic_update_slice_in_dim(
        jnp.zeros_like(branch_term), residual.astype(jnp.float32), feature_first, 1
    )
    stream = lax.psum(branch_term + residual_wide, SEQ)
    square = jnp.sum(stream * stream, axis=1)
    normed = (
        stream * lax.rsqrt(square / stream.shape[1] + norm_epsilon)[:, None] * norm_gain
    ).astype(jnp.bfloat16)
    hidden_out = lax.dynamic_slice_in_dim(stream, feature_first, width_local, 1).astype(
        jnp.bfloat16
    )
    vocab_rows = lm_head.shape[0]
    vocab_first = lax.axis_index(SEQ_BATCH) * vocab_rows
    logits = jnp.einsum(
        "rd,vd->rv",
        lax.all_gather(normed, BATCH, axis=0, tiled=True),
        lm_head,
        preferred_element_type=jnp.float32,
    )
    request_total = parent.shape[0]
    parent_rows = (
        jnp.arange(request_total, dtype=jnp.int32)[:, None] * draft_count + parent
    ).reshape(-1)
    source = logits[parent_rows]
    column = jnp.arange(vocab_rows, dtype=jnp.int32) + vocab_first
    picked = jnp.sum(
        jnp.where(column[None, :] == draft_ids.reshape(-1)[:, None], source, 0.0), axis=1
    )
    local_best = jnp.max(logits, axis=1)
    local_mass = jnp.sum(jnp.exp(logits - local_best[:, None]), axis=1)
    best, exp_mass, chosen = combined_by_axis(
        (local_best, local_mass, picked), SEQ_BATCH, combine_soft
    )
    log_total = best + jnp.log(exp_mass)
    target_all = (chosen - log_total[parent_rows]).reshape(request_total, draft_count)
    target_logp = lax.dynamic_slice_in_dim(target_all, batch_index * requests, requests, 0)
    accepted_score = jnp.sum(
        jnp.where(
            jnp.arange(draft_count, dtype=jnp.int32)[None, :] < accept_len[:, None],
            target_logp,
            0.0,
        ),
        axis=1,
    )
    return (hidden_out, target_logp, accepted_score)


def solution(mesh):
    split = Mesh(mesh.devices.reshape(4, 4, 4, 2), ("seq_0", "seq_1", "batch_0", "batch_1"))
    in_specs = (
        P(BATCH, None, SEQ, None),
        P(BATCH, None, SEQ, None),
        P(SEQ, None, None),
        P(SEQ, None, None),
        P(BATCH, SEQ, None),
        P(BATCH, SEQ, None),
        P(BATCH, None, None),
        P(BATCH, None, None),
        P(BATCH, SEQ),
        P(SEQ, None),
        P(),
        P(SEQ_BATCH, None),
        P(),
        P(),
        P(BATCH),
        P(BATCH),
    )
    out_specs = (P(BATCH, SEQ), P(BATCH, None), P(BATCH))
    return jax.shard_map(body, mesh=split, in_specs=in_specs, out_specs=out_specs, check_vma=False)
```

profile of v0, /device:TPU:1, one launch (start us, length us, event | category | flops | bytes accessed | tf_op | source)
XLA Modules:
  0.0 529.6 jit_solution(17929896783594325636)
XLA Ops:
  14.3 80.4 %all-gather.11.cloned.1.call-done = bf16[1,64,128,576]{3,1,0,2:T(8,128)(2,1)} async-done(((bf16[1,64,8,576]{3,1,0,2:T(8,128)(2,1)}), bf16[1,64,128,576]{3,1,0,2:T(8,128)(2,1)}) %all-gather.11.cloned.1.call-update) | async-done | bytes 9437200 | tf_op jit(solution)/shard_map/all_gather | solution.py:22
  94.7 1.8 split.9
  96.5 2.9 copy.69
  99.4 7.5 %fusion.10 = f32[64,128,64]{0,2,1:T(8,128)S(1)} fusion(bf16[1,64,512]{2,1,0:T(8,128)(2,1)S(1)} %copy-done.5, bf16[1,64,128,576]{3,1,0,2:T(8,128)(2,1)} %all-gather.11.cloned.1.call-done), kind=kOutput, calls=%fused_computation.11 | convolution fusion | flops 536870912 | bytes 10551296 | tf_op jit(solution)/shard_map/rihc,rjc->rhij/dot_general | solution.py:116
  106.9 5.8 %fusion.97 = (f32[128,64]{1,0:T(8,128)S(1)}, f32[1,128,64,64]{2,3,1,0:T(8,128)}) fusion(f32[64,128,64]{0,2,1:T(8,128)S(1)} %fusion.10, bf16[1,64,64]{2,1,0:T(8,128)(2,1)S(1)} %copy-done.8, bf16[1,64,128,576]{3,1,0,2:T(8,128)(2,1)} %all-gather.11.cloned.1.call-done, pred[64,64]{0,1:T(8,128)(4,1)S(1)} %copy.45), kind=kOutput, calls=%fused_computation.169 | convolution fusion | flops 69197824 | bytes 6336512 | tf_op jit(solution)/shard_map/rihe,rje->rhij/dot_general | solution.py:119
  112.8 7.7 %split.8 = bf16[1,64,128,512]{3,1,0,2:T(8,128)(2,1)} slice(bf16[1,64,128,576]{3,1,0,2:T(8,128)(2,1)} %all-gather.11.cloned.1.call-done), slice={[0:1], [0:64], [0:128], [0:512]} | slice | bytes 16777216 | tf_op jit(solution)/shard_map/split | solution.py:22
  120.5 30.0 %fusion.12 = f32[64,128,1024]{2,1,0:T(8,128)} fusion(bf16[1,64,128,512]{3,1,0,2:T(8,128)(2,1)} %split.8, bf16[1,1024,512]{2,1,0:T(8,128)(2,1)S(1)} %copy-done), kind=kOutput, calls=%fused_computation.14 | convolution fusion | flops 8589934592 | bytes 42991616 | tf_op jit(solution)/shard_map/rihc,rtc->rhit/dot_general | solution.py:107
  150.5 21.9 %fusion.96 = (f32[128,64]{0,1:T(8,128)S(1)}, f32[1,128,64,1024]{3,1,2,0:T(8,128)}) fusion(f32[64,128,1024]{2,1,0:T(8,128)} %fusion.12, bf16[1,1024,64]{1,2,0:T(8,128)(2,1)S(1)} %copy-done.4, bf16[1,64,128,64]{2,3,1,0:T(8,128)(2,1)S(1)} %copy-done.3, pred[1024]{0:T(1024)(128)(4,1)S(1)} %add_compare_fusion), kind=kOutput, calls=%fused_computation.168 | convolution fusion | flops 1107288064 | bytes 68322304 | tf_op jit(solution)/shard_map/rihe,rte->rhit/dot_general | solution.py:110
  172.5 15.1 %all_to_all.5 = f32[16,1,128,64]{2,3,1,0:T(8,128)S(1)} all-to-all(f32[16,1,128,64]{2,3,1,0:T(8,128)S(1)} %broadcast_in_dim.37), channel_id=1, replica_groups=mesh['seq_0'=4,'seq_1'=4,'batch_0'=4,'batch_1'=2] {'seq_0','seq_1'}, dimensions={0} | all-to-all | bytes 1048576 | tf_op jit(solution)/shard_map/all_to_all | solution.py:27
  187.7 18.7 %fusion.7 = f32[1,128,64,512]{3,1,2,0:T(8,128)} fusion(f32[1,128,64,1024]{3,1,2,0:T(8,128)} %get-tuple-element.19, f32[128,64]{0,1:T(8,128)S(1)} %reduce_max.38, bf16[1,1024,512]{2,1,0:T(8,128)(2,1)S(1)} %copy-done), kind=kOutput, calls=%fused_computation.10 | convolution fusion | flops 8606711808 | bytes 51412992 | tf_op jit(solution)/shard_map/rhit,rtc->rhic/dot_general | solution.py:129
  209.5 14.9 %fusion.1 = f32[128,64]{0,1:T(8,128)S(1)} fusion(f32[1,128,64,1024]{3,1,2,0:T(8,128)} %get-tuple-element.19, f32[128,64]{0,1:T(8,128)S(1)} %reduce_max.38), kind=kLoop, calls=%fused_computation.5 | loop fusion | flops 16769024 | bytes 33619968 | tf_op jit(solution)/shard_map/reduce_sum | solution.py:128
  224.6 58.5 %all-reduce = f32[1,128,64]{2,1,0:T(8,128)S(1)} all-reduce(f32[1,128,64]{2,1,0:T(8,128)S(1)} %copy.53), channel_id=7, replica_groups=mesh['seq_0'=4,'seq_1'=4,'batch_0'=4,'batch_1'=2] {'seq_0','seq_1'}, use_global_device_ids=true, to_apply=%region_5.6.clone | all-reduce | flops 8192 | bytes 65536
  283.4 33.9 %reduce-scatter.3.cloned.1.call-done = f32[1,8,64,512]{3,1,2,0:T(8,128)} async-done(((f32[1,128,64,512]{3,1,2,0:T(8,128)}), f32[1,8,64,512]{3,1,2,0:T(8,128)}) %reduce-scatter.3.cloned.1.call-update) | async-done | bytes 1048592 | tf_op jit(solution)/shard_map/reduce_scatter | solution.py:146
  319.4 7.9 %fusion.27 = f32[64,7168]{1,0:T(8,128)S(1)} fusion(bf16[1024,7168]{1,0:T(8,128)(2,1)} %param.25, bf16[8,8,8,128]{3,2,1,0:T(8,128)(2,1)S(1)} %bitcast.377), kind=kOutput, calls=%fused_computation.45 | convolution fusion | flops 939524096 | bytes 16646144 | tf_op jit(solution)/shard_map/dot_general | solution.py:157
  329.8 88.2 %all-reduce.3.cloned.1.call-done = f32[64,7168]{1,0:T(8,128)} async-done(((f32[64,7168]{1,0:T(8,128)}), f32[64,7168]{1,0:T(8,128)}) %all-reduce.3.cloned.1.call-update) | async-done | bytes 1835024 | tf_op jit(solution)/shard_map/psum | solution.py:163
  418.0 1.7 multiply_reduce_fusion
  419.7 2.7 multiply_convert_fusion
  425.0 43.8 %all-gather.13.cloned.1.call-done = bf16[512,7168]{1,0:T(8,128)(2,1)} async-done(((bf16[64,7168]{1,0:T(8,128)(2,1)}), bf16[512,7168]{1,0:T(8,128)(2,1)}) %all-gather.13.cloned.1.call-update) | async-done | bytes 7340048 | tf_op jit(solution)/shard_map/all_gather | solution.py:175
  468.8 8.5 %fusion.98 = (f32[512]{0:T(512)S(1)}, f32[512,512]{0,1:T(8,128)S(1)}) fusion(bf16[512,7168]{1,0:T(8,128)(2,1)} %all-gather.13.cloned.1.call-done, bf16[512,7168]{1,0:T(8,128)(2,1)} %param.27), kind=kOutput, calls=%fused_computation.170 | convolution fusion | flops 3758358016 | bytes 15730688 | tf_op jit(solution)/shard_map/rd,vd->rv/dot_general | solution.py:173
  479.7 9.6 %all-gather.4 = f32[4,3,512]{2,1,0:T(4,128)S(1)} all-gather(f32[1,3,512]{2,1,0:T(4,128)S(1)} %maximum_bitcast_fusion.1), channel_id=2, replica_groups=mesh['seq_0'=4,'seq_1'=4,'batch_0'=4,'batch_1'=2] {'seq_0'}, dimensions={0}, use_global_device_ids=true | all-gather | bytes 30720 | tf_op jit(solution)/shard_map/all_gather | solution.py:43
  489.4 9.5 %all-gather.5 = f32[4,3,512]{2,1,0:T(4,128)S(1)} all-gather(f32[1,3,512]{2,1,0:T(4,128)S(1)} %maximum_bitcast_fusion.2), channel_id=3, replica_groups=mesh['seq_0'=4,'seq_1'=4,'batch_0'=4,'batch_1'=2] {'seq_1'}, dimensions={0}, use_global_device_ids=true | all-gather | bytes 30720 | tf_op jit(solution)/shard_map/all_gather | solution.py:43
  498.9 9.0 %all-gather.6 = f32[4,3,512]{2,1,0:T(4,128)S(1)} all-gather(f32[1,3,512]{2,1,0:T(4,128)S(1)} %maximum_bitcast_fusion.3), channel_id=4, replica_groups=mesh['seq_0'=4,'seq_1'=4,'batch_0'=4,'batch_1'=2] {'batch_0'}, dimensions={0}, use_global_device_ids=true | all-gather | bytes 30720 | tf_op jit(solution)/shard_map/all_gather | solution.py:43
  508.0 10.2 %all-gather.7 = f32[2,3,512]{2,1,0:T(4,128)S(1)} all-gather(f32[1,3,512]{2,1,0:T(4,128)S(1)} %maximum_bitcast_fusion.4), channel_id=5, replica_groups=mesh['seq_0'=4,'seq_1'=4,'batch_0'=4,'batch_1'=2] {'batch_1'}, dimensions={0}, use_global_device_ids=true | all-gather | bytes 18432 | tf_op jit(solution)/shard_map/all_gather | solution.py:43
  518.3 3.5 gather_fusion.1
  (101 shorter events, 19.7 us)
Async XLA Ops:
  7.2 113.3 %copy-start = (bf16[1,1024,512]{2,1,0:T(8,128)(2,1)S(1)}, bf16[1,1024,512]{2,1,0:T(8,128)(2,1)}, u32[]{:S(2)}) copy-start(bf16[1,1024,512]{2,1,0:T(8,128)(2,1)} %param.20) | copy-start | bytes 3145732
  7.2 92.3 %copy-start.5 = (bf16[1,64,512]{2,1,0:T(8,128)(2,1)S(1)}, bf16[1,64,512]{2,1,0:T(8,128)(2,1)}, u32[]{:S(2)}) copy-start(bf16[1,64,512]{2,1,0:T(8,128)(2,1)} %param.22) | copy-start | bytes 196612
  7.2 87.5 %all-gather.11.cloned.1.call-start = ((), (), s32[]{:S(2)}) async-start(), calls=%async_computation.2 | async-start | bytes 11141120 | tf_op jit(solution)/shard_map/all_gather | solution.py:22
  10.8 306.5 %reduce-scatter.3.cloned.1.call-start = ((), (), s32[]{:S(2)}) async-start(), calls=%async_computation.3 | async-start | bytes 17825792 | tf_op jit(solution)/shard_map/reduce_scatter | solution.py:146
  96.5 10.4 %copy-start.8 = (bf16[1,64,64]{2,1,0:T(8,128)(2,1)S(1)}, bf16[1,64,64]{2,1,0:T(8,128)(2,1)}, u32[]{:S(2)}) copy-start(bf16[1,64,64]{2,1,0:T(8,128)(2,1)} %param.23) | copy-start | bytes 24580
  120.5 30.0 %copy-start.3 = (bf16[1,64,128,64]{2,3,1,0:T(8,128)(2,1)S(1)}, bf16[1,64,128,64]{2,3,1,0:T(8,128)(2,1)}, u32[]{:S(2)}) copy-start(bf16[1,64,128,64]{2,3,1,0:T(8,128)(2,1)} %copy.69) | copy-start | bytes 3145732
  120.5 30.0 %copy-start.4 = (bf16[1,1024,64]{1,2,0:T(8,128)(2,1)S(1)}, bf16[1,1024,64]{1,2,0:T(8,128)(2,1)}, u32[]{:S(2)}) copy-start(bf16[1,1024,64]{1,2,0:T(8,128)(2,1)} %param.21) | copy-start | bytes 393220
  206.4 0.7 copy-start.12
  206.4 211.5 %all-reduce.3.cloned.1.call-start = ((), (), s32[]{:S(2)}) async-start(), calls=%async_computation.4 | async-start | bytes 3670016 | tf_op jit(solution)/shard_map/psum | solution.py:163
  209.5 109.3 %copy-start.11 = (bf16[8,512,128]{2,1,0:T(8,128)(2,1)S(1)}, bf16[8,512,128]{2,1,0:T(8,128)(2,1)}, u32[]{:S(2)}) copy-start(bf16[8,512,128]{2,1,0:T(8,128)(2,1)} %param.19) | copy-start | bytes 3145732
  319.3 7.9 %copy-start.6 = (bf16[64,448]{1,0:T(8,128)(2,1)S(1)}, bf16[64,448]{1,0:T(8,128)(2,1)}, u32[]{:S(2)}) copy-start(bf16[64,448]{1,0:T(8,128)(2,1)} %param.24) | copy-start | bytes 172036
  319.3 100.3 %copy-start.7 = (f32[7168]{0:T(1024)S(1)}, f32[7168]{0:T(1024)}, u32[]{:S(2)}) copy-start(f32[7168]{0:T(1024)} %param.26) | copy-start | bytes 86020
  319.4 103.7 %copy-start.9 = (s32[8,64]{1,0:T(8,128)S(1)}, s32[8,64]{1,0:T(8,128)}, u32[]{:S(2)}) copy-start(s32[8,64]{1,0:T(8,128)} %param.29) | copy-start | bytes 6148
  319.4 103.8 %copy-start.10 = (s32[8,64]{1,0:T(8,128)S(1)}, s32[8,64]{1,0:T(8,128)}, u32[]{:S(2)}) copy-start(s32[8,64]{1,0:T(8,128)} %param.28) | copy-start | bytes 6148
  328.5 1.3 copy-start.2
  329.7 139.0 %all-gather.13.cloned.1.call-start = ((), (), s32[]{:S(2)}) async-start(), calls=%async_computation.5 | async-start | bytes 8257536 | tf_op jit(solution)/shard_map/all_gather | solution.py:175
  468.8 54.3 %copy-start.1 = (bf16[1,1024,512]{2,1,0:T(8,128)(2,1)S(1)}, bf16[1,1024,512]{2,1,0:T(8,128)(2,1)}, u32[]{:S(2)}) copy-start(bf16[1,1024,512]{2,1,0:T(8,128)(2,1)} %param.20) | copy-start | bytes 3145732
Sparse Core Ops, SparseCore 0:
  10.9 83.7 all-gather.10
  206.5 110.7 reduce-scatter.2
  329.9 88.0 all-reduce.2
  422.5 46.2 all-gather.12
where the time goes:
time: 530 us
  waiting for transfers between devices  246 us (46%)
  blocking collectives  112 us (21%)
  matrix products  106 us (20%)
  local copies, waits for them, and re-layouts  26 us (5%)
  other arithmetic  23.3 us (4%)
  between operations  16.1 us (3%)
    psum x1, waiting for transfers between devices, body(): stream = lax.psum(branch_term + residual_wide, SEQ)  88.2 us
    all_gather x1, waiting for transfers between devices, sent_together(): lax.all_gather(both, axis, axis=dim, tiled=True)  80.4 us
    unnamed x1, blocking collectives  58.5 us
    all_gather x1, waiting for transfers between devices, body(): lax.all_gather(normed, BATCH, axis=0, tiled=True)  43.8 us
    all_gather x4, blocking collectives, gathered_once(): both, at, found = (lax.all_gather(jnp.concatenate(lines), axis), 0, {})  38.3 us
    reduce_scatter x1, waiting for transfers between devices, body(): lax.psum_scatter(partial_value, SEQ, scatter_dimension=1, tiled=True)  33.9 us
    dot_general x1, matrix products, body(): jnp.einsum('rihc,rtc->rhit', query_all, cache_latent, preferred_element_t...  30 us
    dot_general x1, matrix products, body(): jnp.einsum('rihe,rte->rhit', rope_all, cache_rope, preferred_element_type...  21.9 us
  transfers between devices with their start and end apart: 4, of which 4 were waited for; matrix products, arithmetic and copies ran while one was open for 4% of the time, Pallas kernels for 0%

commit v1 on v0

--- a/solution.py
+++ b/solution.py
@@ -4,6 +4,7 @@
 from jax import lax
 from jax.sharding import Mesh
 from jax.sharding import PartitionSpec as P
+from jax.lax import all_to_all, axis_size
 
 SEQ = ("seq_0", "seq_1")
 BATCH = ("batch_0", "batch_1")
@@ -172,7 +173,9 @@
     vocab_first = lax.axis_index(SEQ_BATCH) * vocab_rows
     logits = jnp.einsum(
         "rd,vd->rv",
-        lax.all_gather(normed, BATCH, axis=0, tiled=True),
+        jnp.concatenate(
+            all_to_all(jnp.stack(axis_size(BATCH) * [normed], axis=0), BATCH, 0, 0), axis=0
+        ),
         lm_head,
         preferred_element_type=jnp.float32,
     )

time: 530 us -> 576 us (1.087)
  waiting for transfers between devices: 246 us -> 283 us
  starting transfers between devices: 0.16 us -> 6.97 us
    all_to_all x0 -> x1, waiting for transfers between devices: none -> 80.1 us  [body(): all_to_all(jnp.stack(axis_size(BATCH) * [normed], axis=0), BATCH, 0, 0)]
    all_gather x1 -> x0, waiting for transfers between devices: 43.8 us -> none  [body(): lax.all_gather(normed, BATCH, axis=0, tiled=True)]
    all_to_all x0 -> x1, starting transfers between devices: none -> 6.85 us  [body(): all_to_all(jnp.stack(axis_size(BATCH) * [normed], axis=0), BATCH, 0, 0)]
where the time goes in v1:
time: 576 us; the launch traced here: 575 us
  waiting for transfers between devices  283 us (49%)
  blocking collectives  112 us (19%)
  matrix products  106 us (18%)
  local copies, waits for them, and re-layouts  29.9 us (5%)
  other arithmetic  22.4 us (4%)
  between operations  16.1 us (3%)
  starting transfers between devices  6.97 us (1%)
    psum x1, waiting for transfers between devices, body(): stream = lax.psum(branch_term + residual_wide, SEQ)  88.1 us
    all_gather x1, waiting for transfers between devices, sent_together(): lax.all_gather(both, axis, axis=dim, tiled=True)  80.4 us
    all_to_all x1, waiting for transfers between devices, body(): all_to_all(jnp.stack(axis_size(BATCH) * [normed], axis=0), BATCH, 0, 0)  80.1 us
    unnamed x1, blocking collectives  58.5 us
    all_gather x4, blocking collectives, gathered_once(): both, at, found = (lax.all_gather(jnp.concatenate(lines), axis), 0, {})  38.1 us
    reduce_scatter x1, waiting for transfers between devices, body(): lax.psum_scatter(partial_value, SEQ, scatter_dimension=1, tiled=True)  34 us
    dot_general x1, matrix products, body(): jnp.einsum('rihc,rtc->rhit', query_all, cache_latent, preferred_element_t...  30 us
    dot_general x1, matrix products, body(): jnp.einsum('rihe,rte->rhit', rope_all, cache_rope, preferred_element_type...  21.9 us
  transfers between devices with their start and end apart: 4, of which 4 were waited for; matrix products, arithmetic and copies ran while one was open for 4% of the time, Pallas kernels for 0%

profile of v1, /device:TPU:1, one launch (start us, length us, event | category | flops | bytes accessed | tf_op | source)
XLA Modules:
  0.0 575.4 jit_solution(11403676779518332142)
XLA Ops:
  14.3 80.4 %all-gather.10.cloned.1.call-done = bf16[1,64,128,576]{3,1,0,2:T(8,128)(2,1)} async-done(((bf16[1,64,8,576]{3,1,0,2:T(8,128)(2,1)}), bf16[1,64,128,576]{3,1,0,2:T(8,128)(2,1)}) %all-gather.10.cloned.1.call-update) | async-done | bytes 9437200 | tf_op jit(solution)/shard_map/all_gather | solution.py:23
  94.7 1.8 split.9
  96.5 2.9 copy.69
  99.4 7.5 %fusion.10 = f32[64,128,64]{0,2,1:T(8,128)S(1)} fusion(bf16[1,64,512]{2,1,0:T(8,128)(2,1)S(1)} %copy-done.5, bf16[1,64,128,576]{3,1,0,2:T(8,128)(2,1)} %all-gather.10.cloned.1.call-done), kind=kOutput, calls=%fused_computation.11 | convolution fusion | flops 536870912 | bytes 10551296 | tf_op jit(solution)/shard_map/rihc,rjc->rhij/dot_general | solution.py:117
  106.9 5.8 %fusion.97 = (f32[128,64]{1,0:T(8,128)S(1)}, f32[1,128,64,64]{2,3,1,0:T(8,128)}) fusion(f32[64,128,64]{0,2,1:T(8,128)S(1)} %fusion.10, bf16[1,64,64]{2,1,0:T(8,128)(2,1)S(1)} %copy-done.8, bf16[1,64,128,576]{3,1,0,2:T(8,128)(2,1)} %all-gather.10.cloned.1.call-done, pred[64,64]{0,1:T(8,128)(4,1)S(1)} %copy.45), kind=kOutput, calls=%fused_computation.169 | convolution fusion | flops 69197824 | bytes 6336512 | tf_op jit(solution)/shard_map/rihe,rje->rhij/dot_general | solution.py:120
  112.8 7.7 %split.8 = bf16[1,64,128,512]{3,1,0,2:T(8,128)(2,1)} slice(bf16[1,64,128,576]{3,1,0,2:T(8,128)(2,1)} %all-gather.10.cloned.1.call-done), slice={[0:1], [0:64], [0:128], [0:512]} | slice | bytes 16777216 | tf_op jit(solution)/shard_map/split | solution.py:23
  120.5 30.0 %fusion.12 = f32[64,128,1024]{2,1,0:T(8,128)} fusion(bf16[1,64,128,512]{3,1,0,2:T(8,128)(2,1)} %split.8, bf16[1,1024,512]{2,1,0:T(8,128)(2,1)S(1)} %copy-done), kind=kOutput, calls=%fused_computation.14 | convolution fusion | flops 8589934592 | bytes 42991616 | tf_op jit(solution)/shard_map/rihc,rtc->rhit/dot_general | solution.py:108
  150.5 21.9 %fusion.96 = (f32[128,64]{0,1:T(8,128)S(1)}, f32[1,128,64,1024]{3,1,2,0:T(8,128)}) fusion(f32[64,128,1024]{2,1,0:T(8,128)} %fusion.12, bf16[1,1024,64]{1,2,0:T(8,128)(2,1)S(1)} %copy-done.4, bf16[1,64,128,64]{2,3,1,0:T(8,128)(2,1)S(1)} %copy-done.3, pred[1024]{0:T(1024)(128)(4,1)S(1)} %add_compare_fusion), kind=kOutput, calls=%fused_computation.168 | convolution fusion | flops 1107288064 | bytes 68322304 | tf_op jit(solution)/shard_map/rihe,rte->rhit/dot_general | solution.py:111
  172.5 15.1 %all_to_all.10 = f32[16,1,128,64]{2,3,1,0:T(8,128)S(1)} all-to-all(f32[16,1,128,64]{2,3,1,0:T(8,128)S(1)} %broadcast_in_dim.37), channel_id=1, replica_groups=mesh['seq_0'=4,'seq_1'=4,'batch_0'=4,'batch_1'=2] {'seq_0','seq_1'}, dimensions={0} | all-to-all | bytes 1048576 | tf_op jit(solution)/shard_map/all_to_all | solution.py:28
  187.7 18.7 %fusion.7 = f32[1,128,64,512]{3,1,2,0:T(8,128)} fusion(f32[1,128,64,1024]{3,1,2,0:T(8,128)} %get-tuple-element.19, f32[128,64]{0,1:T(8,128)S(1)} %reduce_max.38, bf16[1,1024,512]{2,1,0:T(8,128)(2,1)S(1)} %copy-done), kind=kOutput, calls=%fused_computation.10 | convolution fusion | flops 8606711808 | bytes 51412992 | tf_op jit(solution)/shard_map/rhit,rtc->rhic/dot_general | solution.py:130
  209.5 14.9 %fusion.1 = f32[128,64]{0,1:T(8,128)S(1)} fusion(f32[1,128,64,1024]{3,1,2,0:T(8,128)} %get-tuple-element.19, f32[128,64]{0,1:T(8,128)S(1)} %reduce_max.38), kind=kLoop, calls=%fused_computation.5 | loop fusion | flops 16769024 | bytes 33619968 | tf_op jit(solution)/shard_map/reduce_sum | solution.py:129
  224.6 58.5 %all-reduce = f32[1,128,64]{2,1,0:T(8,128)S(1)} all-reduce(f32[1,128,64]{2,1,0:T(8,128)S(1)} %copy.53), channel_id=7, replica_groups=mesh['seq_0'=4,'seq_1'=4,'batch_0'=4,'batch_1'=2] {'seq_0','seq_1'}, use_global_device_ids=true, to_apply=%region_5.6.clone | all-reduce | flops 8192 | bytes 65536
  283.4 34.0 %reduce-scatter.3.cloned.1.call-done = f32[1,8,64,512]{3,1,2,0:T(8,128)} async-done(((f32[1,128,64,512]{3,1,2,0:T(8,128)}), f32[1,8,64,512]{3,1,2,0:T(8,128)}) %reduce-scatter.3.cloned.1.call-update) | async-done | bytes 1048592 | tf_op jit(solution)/shard_map/reduce_scatter | solution.py:147
  319.4 7.9 %fusion.27 = f32[64,7168]{1,0:T(8,128)S(1)} fusion(bf16[1024,7168]{1,0:T(8,128)(2,1)} %param.25, bf16[8,8,8,128]{3,2,1,0:T(8,128)(2,1)S(1)} %bitcast.378), kind=kOutput, calls=%fused_computation.45 | convolution fusion | flops 939524096 | bytes 16646144 | tf_op jit(solution)/shard_map/dot_general | solution.py:158
  329.8 88.1 %all-reduce.3.cloned.1.call-done = f32[64,7168]{1,0:T(8,128)} async-done(((f32[64,7168]{1,0:T(8,128)}), f32[64,7168]{1,0:T(8,128)}) %all-reduce.3.cloned.1.call-update) | async-done | bytes 1835024 | tf_op jit(solution)/shard_map/psum | solution.py:164
  421.4 3.9 stack.2
  425.3 6.9 %all-to-all-start.1 = ((bf16[8,64,7168]{2,1,0:T(8,128)(2,1)}), bf16[8,64,7168]{2,1,0:T(8,128)(2,1)}, u32[]{:S(2)}, u32[]{:S(2)}) async-start(bf16[8,64,7168]{2,1,0:T(8,128)(2,1)} %stack.2), calls=%async_computation.2 | async-start | bytes 14680064 | tf_op jit(solution)/shard_map/all_to_all | solution.py:177
  434.7 80.1 %all-to-all-done.1 = bf16[8,64,7168]{2,1,0:T(8,128)(2,1)} async-done(((bf16[8,64,7168]{2,1,0:T(8,128)(2,1)}), bf16[8,64,7168]{2,1,0:T(8,128)(2,1)}, u32[]{:S(2)}, u32[]{:S(2)}) %all-to-all-start.1) | async-done | bytes 7340064 | tf_op jit(solution)/shard_map/all_to_all | solution.py:177
  514.8 8.5 %fusion.98 = (f32[512]{0:T(512)S(1)}, f32[512,512]{0,1:T(8,128)S(1)}) fusion(bf16[512,7168]{1,0:T(8,128)(2,1)} %bitcast.35, bf16[512,7168]{1,0:T(8,128)(2,1)} %param.27), kind=kOutput, calls=%fused_computation.170 | convolution fusion | flops 3758358016 | bytes 15730688 | tf_op jit(solution)/shard_map/rd,vd->rv/dot_general | solution.py:174
  525.8 9.0 %all-gather.4 = f32[4,3,512]{2,1,0:T(4,128)S(1)} all-gather(f32[1,3,512]{2,1,0:T(4,128)S(1)} %maximum_bitcast_fusion.1), channel_id=2, replica_groups=mesh['seq_0'=4,'seq_1'=4,'batch_0'=4,'batch_1'=2] {'seq_0'}, dimensions={0}, use_global_device_ids=true | all-gather | bytes 30720 | tf_op jit(solution)/shard_map/all_gather | solution.py:44
  534.9 9.0 %all-gather.5 = f32[4,3,512]{2,1,0:T(4,128)S(1)} all-gather(f32[1,3,512]{2,1,0:T(4,128)S(1)} %maximum_bitcast_fusion.2), channel_id=3, replica_groups=mesh['seq_0'=4,'seq_1'=4,'batch_0'=4,'batch_1'=2] {'seq_1'}, dimensions={0}, use_global_device_ids=true | all-gather | bytes 30720 | tf_op jit(solution)/shard_map/all_gather | solution.py:44
  544.0 9.0 %all-gather.6 = f32[4,3,512]{2,1,0:T(4,128)S(1)} all-gather(f32[1,3,512]{2,1,0:T(4,128)S(1)} %maximum_bitcast_fusion.3), channel_id=4, replica_groups=mesh['seq_0'=4,'seq_1'=4,'batch_0'=4,'batch_1'=2] {'batch_0'}, dimensions={0}, use_global_device_ids=true | all-gather | bytes 30720 | tf_op jit(solution)/shard_map/all_gather | solution.py:44
  553.1 11.0 %all-gather.7 = f32[2,3,512]{2,1,0:T(4,128)S(1)} all-gather(f32[1,3,512]{2,1,0:T(4,128)S(1)} %maximum_bitcast_fusion.4), channel_id=5, replica_groups=mesh['seq_0'=4,'seq_1'=4,'batch_0'=4,'batch_1'=2] {'batch_1'}, dimensions={0}, use_global_device_ids=true | all-gather | bytes 18432 | tf_op jit(solution)/shard_map/all_gather | solution.py:44
  564.1 3.5 gather_fusion.1
  (101 shorter events, 23.0 us)
Async XLA Ops:
  7.2 113.3 %copy-start = (bf16[1,1024,512]{2,1,0:T(8,128)(2,1)S(1)}, bf16[1,1024,512]{2,1,0:T(8,128)(2,1)}, u32[]{:S(2)}) copy-start(bf16[1,1024,512]{2,1,0:T(8,128)(2,1)} %param.20) | copy-start | bytes 3145732
  7.2 92.3 %copy-start.5 = (bf16[1,64,512]{2,1,0:T(8,128)(2,1)S(1)}, bf16[1,64,512]{2,1,0:T(8,128)(2,1)}, u32[]{:S(2)}) copy-start(bf16[1,64,512]{2,1,0:T(8,128)(2,1)} %param.22) | copy-start | bytes 196612
  7.2 87.5 %all-gather.10.cloned.1.call-start = ((), (), s32[]{:S(2)}) async-start(), calls=%async_computation.3 | async-start | bytes 11141120 | tf_op jit(solution)/shard_map/all_gather | solution.py:23
  10.8 306.6 %reduce-scatter.3.cloned.1.call-start = ((), (), s32[]{:S(2)}) async-start(), calls=%async_computation.4 | async-start | bytes 17825792 | tf_op jit(solution)/shard_map/reduce_scatter | solution.py:147
  96.5 10.4 %copy-start.8 = (bf16[1,64,64]{2,1,0:T(8,128)(2,1)S(1)}, bf16[1,64,64]{2,1,0:T(8,128)(2,1)}, u32[]{:S(2)}) copy-start(bf16[1,64,64]{2,1,0:T(8,128)(2,1)} %param.23) | copy-start | bytes 24580
  120.5 30.0 %copy-start.3 = (bf16[1,64,128,64]{2,3,1,0:T(8,128)(2,1)S(1)}, bf16[1,64,128,64]{2,3,1,0:T(8,128)(2,1)}, u32[]{:S(2)}) copy-start(bf16[1,64,128,64]{2,3,1,0:T(8,128)(2,1)} %copy.69) | copy-start | bytes 3145732
  120.5 30.0 %copy-start.4 = (bf16[1,1024,64]{1,2,0:T(8,128)(2,1)S(1)}, bf16[1,1024,64]{1,2,0:T(8,128)(2,1)}, u32[]{:S(2)}) copy-start(bf16[1,1024,64]{1,2,0:T(8,128)(2,1)} %param.21) | copy-start | bytes 393220
  206.4 0.7 copy-start.12
  206.4 211.5 %all-reduce.3.cloned.1.call-start = ((), (), s32[]{:S(2)}) async-start(), calls=%async_computation.5 | async-start | bytes 3670016 | tf_op jit(solution)/shard_map/psum | solution.py:164
  209.5 109.4 %copy-start.11 = (bf16[8,512,128]{2,1,0:T(8,128)(2,1)S(1)}, bf16[8,512,128]{2,1,0:T(8,128)(2,1)}, u32[]{:S(2)}) copy-start(bf16[8,512,128]{2,1,0:T(8,128)(2,1)} %param.19) | copy-start | bytes 3145732
  319.4 7.9 %copy-start.6 = (bf16[64,448]{1,0:T(8,128)(2,1)S(1)}, bf16[64,448]{1,0:T(8,128)(2,1)}, u32[]{:S(2)}) copy-start(bf16[64,448]{1,0:T(8,128)(2,1)} %param.24) | copy-start | bytes 172036
  319.4 100.2 %copy-start.7 = (f32[7168]{0:T(1024)S(1)}, f32[7168]{0:T(1024)}, u32[]{:S(2)}) copy-start(f32[7168]{0:T(1024)} %param.26) | copy-start | bytes 86020
  328.5 1.3 copy-start.2
  425.3 7.5 %copy-start.9 = (s32[8,64]{1,0:T(8,128)S(1)}, s32[8,64]{1,0:T(8,128)}, u32[]{:S(2)}) copy-start(s32[8,64]{1,0:T(8,128)} %param.29) | copy-start | bytes 6148
  425.3 7.6 %copy-start.10 = (s32[8,64]{1,0:T(8,128)S(1)}, s32[8,64]{1,0:T(8,128)}, u32[]{:S(2)}) copy-start(s32[8,64]{1,0:T(8,128)} %param.28) | copy-start | bytes 6148
  425.3 89.5 %all-to-all-start.1 = ((bf16[8,64,7168]{2,1,0:T(8,128)(2,1)}), bf16[8,64,7168]{2,1,0:T(8,128)(2,1)}, u32[]{:S(2)}, u32[]{:S(2)}) async-start(bf16[8,64,7168]{2,1,0:T(8,128)(2,1)} %stack.2), calls=%async_computation.2 | async-start | bytes 14680064 | tf_op jit(solution)/shard_map/all_to_all | solution.py:177
  514.8 54.1 %copy-start.1 = (bf16[1,1024,512]{2,1,0:T(8,128)(2,1)S(1)}, bf16[1,1024,512]{2,1,0:T(8,128)(2,1)}, u32[]{:S(2)}) copy-start(bf16[1,1024,512]{2,1,0:T(8,128)(2,1)} %param.20) | copy-start | bytes 3145732
Sparse Core Ops, SparseCore 0:
  10.9 83.7 all-gather.9
  206.5 110.8 reduce-scatter.2
  329.9 87.9 all-reduce.2
